TPU v7x, 32 devices: a whole 2x2x4 slice. The times are simulated.
32 devices in a mesh: clips: 2 (over y), frame: 4 (over z), row: 2 (over x), head: 2 (over core).
Axes of the slice: x: 2, y: 2, z: 4, core: 2. Of those that a mesh axis runs over, the one named last changes fastest.
Arguments:
- query: bfloat16 [64, 16, 8, 1536], P(('clips', 'frame'), 'row', None, 'head'), parts along dimension 0, may hold values from -7 to 7
- keys: bfloat16 [64, 16, 8, 1536], P(('clips', 'frame'), 'row', None, 'head'), parts along dimension 0, may hold values from -6 to 6
- values: bfloat16 [64, 16, 8, 1536], P(('clips', 'frame'), 'row', None, 'head'), parts along dimension 0, may hold values from -6 to 6
Outputs:
- attended: bfloat16 [64, 16, 8, 1536], P(('clips', 'frame'), 'row', None, 'head'), parts along dimension 0
There are 2 independent parts, one for each index of `clips`. A program takes and returns all parts, laid end to end along the dimension named above; each array names one. Nothing has to cross between parts.
All inputs are finite; a program needn't handle non-finite values.
Results may differ from a plain program's by a relative error of at most 0.0047.
Values may be sent and summed in bfloat16 or wider, within the bound.
A program may use at most 64 MiB of HBM per device.

v0:
```python
import math

import jax
import jax.numpy as jnp
from jax import lax
from jax.sharding import PartitionSpec as P

HD = 128
TF = 4
TR = 8
TC = 8


def padded(cells, sides, width):
    for axis, dim in sides:
        count = lax.axis_size(axis)
        ends = count - 1
        head = lax.slice_in_dim(cells, 0, width, axis=dim)
        tail = lax.slice_in_dim(cells, cells.shape[dim] - width, cells.shape[dim], axis=dim)
        cells = jnp.concatenate(
            [
                lax.ppermute(tail, axis, [(i, (i + 1) % count) for i in range(ends)]),
                cells,
                lax.ppermute(head, axis, [((i + 1) % count, i) for i in range(ends)]),
            ],
            axis=dim,
        )
    return cells


def per_device(query, keys, values):
    features = query.shape[3]
    columns = query.shape[2]
    heads_here = features // HD
    tile_size = TF * TR * TC
    column_tiles = columns // TC
    block_rows = column_tiles * tile_size
    score_scale = 1.0 / math.sqrt(HD)
    stacked = jnp.stack((keys, values), 0).reshape(2, 2, TF, 1, TR, columns, features)
    extended = padded(stacked, (("frame", 1), ("row", 3)), 1)
    frame_index = lax.axis_index("frame")
    row_index = lax.axis_index("row")
    frame_count = lax.axis_size("frame")
    count_of_rows = lax.axis_size("row")
    offsets = jnp.arange(3, dtype=jnp.int32) - 1
    tile_frames = 2 * frame_index + jnp.arange(2, dtype=jnp.int32)[:, None] + offsets[None, :]
    frame_ok = (tile_frames >= 0) & (tile_frames < 2 * frame_count)
    tile_rows = row_index + offsets
    row_ok = (tile_rows >= 0) & (tile_rows < count_of_rows)
    tile_mask = frame_ok[:, :, None] & row_ok[None, None, :]
    allowed = jnp.broadcast_to(tile_mask[:, None, :, :, None], (2, block_rows, 3, 3, block_rows))
    allowed = allowed.reshape(2, block_rows, 9 * block_rows)
    tiled_queries = query.reshape(2, TF, TR, column_tiles, TC, features).transpose(0, 3, 1, 2, 4, 5)
    tiled_queries = tiled_queries.reshape(2, block_rows, features)

    def one_head(head_index):
        start = head_index * HD
        head_queries = lax.dynamic_slice_in_dim(tiled_queries, start, HD, 2)
        head_grid = lax.dynamic_slice_in_dim(extended, start, HD, 6)
        key_groups = jnp.stack((head_grid[:, 0:3], head_grid[:, 1:4]), 1)
        key_groups = key_groups.reshape(2, 2, 3, TF, 3, TR, column_tiles, TC, HD)
        key_groups = key_groups.transpose(0, 1, 2, 4, 6, 3, 5, 7, 8).reshape(
            2, 2, 9 * block_rows, HD
        )
        scores = (
            jnp.einsum(
                "jyh,jvh->jyv", head_queries, key_groups[0], preferred_element_type=jnp.float32
            )
            * score_scale
        )
        scores = jnp.where(allowed, scores, -jnp.inf)
        row_peak = jnp.max(scores, axis=-1, keepdims=True)
        weights = jnp.exp(scores - row_peak)
        row_total = jnp.sum(weights, axis=-1, keepdims=True)
        rounded_length = weights.astype(jnp.bfloat16)
        summed = jnp.einsum(
            "git,gth->gih", rounded_length, key_groups[1], preferred_element_type=jnp.float32
        )
        return (summed / row_total).astype(jnp.bfloat16)

    head_results = lax.map(one_head, jnp.arange(heads_here, dtype=jnp.int32))
    attention_output = head_results.transpose(1, 2, 0, 3).reshape(
        2, column_tiles, TF, TR, TC, features
    )
    return attention_output.transpose(0, 2, 3, 1, 4, 5).reshape(2 * TF, TR, columns, features)


def solution(mesh):
    return jax.shard_map(
        per_device,
        mesh=mesh,
        in_specs=(
            P(("clips", "frame"), "row", None, "head"),
            P(("clips", "frame"), "row", None, "head"),
            P(("clips", "frame"), "row", None, "head"),
        ),
        out_specs=P(("clips", "frame"), "row", None, "head"),
        check_vma=False,
    )
```

profile of v0, /device:TPU:0, one launch (start us, length us, event | category | flops | bytes accessed | tf_op | source)
XLA Modules:
  0.0 165.7 jit_solution(2696380435267602327)
XLA Ops:
  0.0 0.0 copy-start
  0.0 0.0 copy-start.1
  0.0 1.6 fusion.22
  1.6 5.0 %collective-permute-start = (bf16[2,1,4,1,8,8,768]{6,5,4,2,3,1,0:T(8,128)(2,1)S(1)}, bf16[2,1,4,1,8,8,768]{6,5,4,2,3,1,0:T(8,128)(2,1)S(1)}, u32[]{:S(2)}, u32[]{:S(2)}) collective-permute-start(bf16[2,1,4,1,8,8,768]{6,5,4,2,3,1,0:T(8,128)(2,1)S(1)} %get-tuple-element.71), channel_id=1, source_target_pairs={{0,4},{4,8},{8,12},{1,5},{5,9},{9,13},{2,6},{6,10},{10,14},{3,7},{... | collective-permute-start | bytes 2359304 | tf_op jit(solution)/shard_map/ppermute | solution.py:22
  6.6 1.3 collective-permute-start.1
  7.9 15.4 %collective-permute-done = bf16[2,1,4,1,8,8,768]{6,5,4,2,3,1,0:T(8,128)(2,1)S(1)} collective-permute-done((bf16[2,1,4,1,8,8,768]{6,5,4,2,3,1,0:T(8,128)(2,1)S(1)}, bf16[2,1,4,1,8,8,768]{6,5,4,2,3,1,0:T(8,128)(2,1)S(1)}, u32[]{:S(2)}, u32[]{:S(2)}) %collective-permute-start) | collective-permute-done | bytes 786464 | tf_op jit(solution)/shard_map/ppermute | solution.py:22
  23.4 4.2 %collective-permute-done.1 = bf16[2,1,4,1,8,8,768]{6,5,4,2,3,1,0:T(8,128)(2,1)S(1)} collective-permute-done((bf16[2,1,4,1,8,8,768]{6,5,4,2,3,1,0:T(8,128)(2,1)S(1)}, bf16[2,1,4,1,8,8,768]{6,5,4,2,3,1,0:T(8,128)(2,1)S(1)}, u32[]{:S(2)}, u32[]{:S(2)}) %collective-permute-start.1) | collective-permute-done | bytes 786464 | tf_op jit(solution)/shard_map/ppermute | solution.py:24
  27.5 0.0 copy-done
  27.5 0.0 copy-done.1
  27.5 1.8 %pad_maximum_fusion.1 = bf16[2,4,4,1,8,8,768]{6,5,4,2,3,1,0:T(8,128)(2,1)} fusion(bf16[2,1,4,1,8,8,768]{6,5,4,2,3,1,0:T(8,128)(2,1)S(1)} %collective-permute-done.1, bf16[1,2,4,1,8,8,768]{6,5,4,2,3,1,0:T(8,128)(2,1)S(1)} %bitcast.43, bf16[1,2,4,1,8,8,768]{6,5,4,2,3,1,0:T(8,128)(2,1)S(1)} %bitcast.40, ...), kind=kLoop, calls=%fused_computation.18 | loop fusion | flops 4718592 | bytes 6291456 | tf_op jit(solution)/shard_map/concatenate | solution.py:20
  29.4 5.0 %collective-permute-start.2 = (bf16[2,4,4,1,8,8,768]{6,5,4,2,3,1,0:T(8,128)(2,1)}, bf16[2,4,4,1,8,8,768]{6,5,4,2,3,1,0:T(8,128)(2,1)}, u32[]{:S(2)}, u32[]{:S(2)}) collective-permute-start(bf16[2,4,4,1,8,8,768]{6,5,4,2,3,1,0:T(8,128)(2,1)} %pad_maximum_fusion.1), channel_id=1, source_target_pairs={{0,2},{1,3},{4,6},{5,7},{8,10},{9,11},{12,14},{13,15},{16,18},{17,... | collective-permute-start | bytes 9437192 | tf_op jit(solution)/shard_map/ppermute | solution.py:22
  34.4 1.3 collective-permute-start.3
  35.7 0.1 compare_and_fusion.1
  35.8 0.1 broadcast_and_fusion
  35.9 0.1 broadcast_in_dim.28
  36.0 63.3 %collective-permute-done.2 = bf16[2,4,4,1,8,8,768]{6,5,4,2,3,1,0:T(8,128)(2,1)} collective-permute-done((bf16[2,4,4,1,8,8,768]{6,5,4,2,3,1,0:T(8,128)(2,1)}, bf16[2,4,4,1,8,8,768]{6,5,4,2,3,1,0:T(8,128)(2,1)}, u32[]{:S(2)}, u32[]{:S(2)}) %collective-permute-start.2) | collective-permute-done | bytes 3145760 | tf_op jit(solution)/shard_map/ppermute | solution.py:22
  99.3 5.7 %collective-permute-done.3 = bf16[2,4,4,1,8,8,768]{6,5,4,2,3,1,0:T(8,128)(2,1)} collective-permute-done((bf16[2,4,4,1,8,8,768]{6,5,4,2,3,1,0:T(8,128)(2,1)}, bf16[2,4,4,1,8,8,768]{6,5,4,2,3,1,0:T(8,128)(2,1)}, u32[]{:S(2)}, u32[]{:S(2)}) %collective-permute-start.3) | collective-permute-done | bytes 3145760 | tf_op jit(solution)/shard_map/ppermute | solution.py:24
  105.0 7.0 %pad_maximum_fusion = bf16[2,4,4,3,8,8,768]{6,5,4,2,3,1,0:T(8,128)(2,1)} fusion(bf16[2,4,4,1,8,8,768]{6,5,4,2,3,1,0:T(8,128)(2,1)} %collective-permute-done.3, bf16[2,1,4,1,8,8,768]{6,5,4,2,3,1,0:T(8,128)(2,1)S(1)} %collective-permute-done.1, bf16[1,2,4,1,8,8,768]{6,5,4,2,3,1,0:T(8,128)(2,1)S(1)} %bitcast.44, ...), kind=kLoop, calls=%fused_computation.17 | loop fusion | flops 23592960 | bytes 18874368 | tf_op jit(solution)/shard_map/concatenate | solution.py:20
  112.0 50.2 %while.11 = (s32[]{:T(128)}, bf16[6,2,256,128]{3,2,1,0:T(8,128)(2,1)}, s32[6]{0:T(128)S(1)}, bf16[2,256,768]{2,1,0:T(8,128)(2,1)}, bf16[2,4,4,3,8,8,768]{6,5,4,2...) while((s32[]{:T(128)}, ...), condition=%wide.region_3.4_spmd.clone, body=%wide.region_0.3_spmd.clone.sunk | while | flops 613547008 | bytes 30948544 | solution.py:81
  112.0 0.6 dynamic_slice.20
  113.2 2.2 %dynamic-slice_bitcast_fusion.3 = (bf16[2,1,3,4,3,8,8,128]{7,6,5,3,4,2,0,1:T(8,128)(2,1)S(1)}, bf16[2,1,3,4,3,8,8,128]{7,6,5,3,4,2,0,1:T(8,128)(2,1)S(1)}) fusion(bf16[2,4,4,3,8,8,768]{6,5,4,2,3,1,0:T(8,128)(2,1)} %get-tuple-element.148, s32[]{:T(128)S(6)} %select_n.12, s32[]{:T(128)S(6)} %add.76), kind=kLoop, calls=%fused_computation.10.clone.1 | loop fusion | bytes 4718600 | tf_op jit(solution)/shard_map/while/body/eval_jaxpr/stack | solution.py:60
  115.3 0.2 maximum_bitcast_fusion.2
  115.6 0.6 fusion.37
  116.2 1.8 %fusion.38 = (f32[2,256]{1,0:T(2,128)S(1)}, f32[2,256,2304]{2,1,0:T(8,128)S(1)}) fusion(bf16[2,2304,128]{2,1,0:T(8,128)(2,1)S(1)} %bitcast.37, bf16[2,256,768]{2,1,0:T(8,128)(2,1)} %get-tuple-element.147, s32[]{:T(128)S(6)} %select_n.12, pred[2,2304]{1,0:T(4,128)(4,1)S(1)} %get-tuple-element.149), kind=kOutput, calls=%fused_computation.29.clone.1 | convolution fusion | flops 305528320 | bytes 6035972 | tf_op jit(solution)/shard_map/while/body/eval_jaxpr/jyh,jvh->jyv/dot_general | solution.py:66
  118.0 0.8 fusion.39
  118.7 1.6 fusion.40
  120.4 0.6 dynamic_slice.20
  121.5 2.2 %dynamic-slice_bitcast_fusion.3 = (bf16[2,1,3,4,3,8,8,128]{7,6,5,3,4,2,0,1:T(8,128)(2,1)S(1)}, bf16[2,1,3,4,3,8,8,128]{7,6,5,3,4,2,0,1:T(8,128)(2,1)S(1)}) fusion(bf16[2,4,4,3,8,8,768]{6,5,4,2,3,1,0:T(8,128)(2,1)} %get-tuple-element.148, s32[]{:T(128)S(6)} %select_n.12, s32[]{:T(128)S(6)} %add.76), kind=kLoop, calls=%fused_computation.10.clone.1 | loop fusion | bytes 4718600 | tf_op jit(solution)/shard_map/while/body/eval_jaxpr/stack | solution.py:60
  123.7 0.2 maximum_bitcast_fusion.2
  123.9 0.6 fusion.37
  124.5 1.8 %fusion.38 = (f32[2,256]{1,0:T(2,128)S(1)}, f32[2,256,2304]{2,1,0:T(8,128)S(1)}) fusion(bf16[2,2304,128]{2,1,0:T(8,128)(2,1)S(1)} %bitcast.37, bf16[2,256,768]{2,1,0:T(8,128)(2,1)} %get-tuple-element.147, s32[]{:T(128)S(6)} %select_n.12, pred[2,2304]{1,0:T(4,128)(4,1)S(1)} %get-tuple-element.149), kind=kOutput, calls=%fused_computation.29.clone.1 | convolution fusion | flops 305528320 | bytes 6035972 | tf_op jit(solution)/shard_map/while/body/eval_jaxpr/jyh,jvh->jyv/dot_general | solution.py:66
  126.3 0.8 fusion.39
  127.1 1.6 fusion.40
  128.7 0.6 dynamic_slice.20
  129.9 2.2 %dynamic-slice_bitcast_fusion.3 = (bf16[2,1,3,4,3,8,8,128]{7,6,5,3,4,2,0,1:T(8,128)(2,1)S(1)}, bf16[2,1,3,4,3,8,8,128]{7,6,5,3,4,2,0,1:T(8,128)(2,1)S(1)}) fusion(bf16[2,4,4,3,8,8,768]{6,5,4,2,3,1,0:T(8,128)(2,1)} %get-tuple-element.148, s32[]{:T(128)S(6)} %select_n.12, s32[]{:T(128)S(6)} %add.76), kind=kLoop, calls=%fused_computation.10.clone.1 | loop fusion | bytes 4718600 | tf_op jit(solution)/shard_map/while/body/eval_jaxpr/stack | solution.py:60
  132.1 0.2 maximum_bitcast_fusion.2
  132.3 0.6 fusion.37
  132.9 1.8 %fusion.38 = (f32[2,256]{1,0:T(2,128)S(1)}, f32[2,256,2304]{2,1,0:T(8,128)S(1)}) fusion(bf16[2,2304,128]{2,1,0:T(8,128)(2,1)S(1)} %bitcast.37, bf16[2,256,768]{2,1,0:T(8,128)(2,1)} %get-tuple-element.147, s32[]{:T(128)S(6)} %select_n.12, pred[2,2304]{1,0:T(4,128)(4,1)S(1)} %get-tuple-element.149), kind=kOutput, calls=%fused_computation.29.clone.1 | convolution fusion | flops 305528320 | bytes 6035972 | tf_op jit(solution)/shard_map/while/body/eval_jaxpr/jyh,jvh->jyv/dot_general | solution.py:66
  134.7 0.8 fusion.39
  135.5 1.6 fusion.40
  137.1 0.6 dynamic_slice.20
  138.2 2.2 %dynamic-slice_bitcast_fusion.3 = (bf16[2,1,3,4,3,8,8,128]{7,6,5,3,4,2,0,1:T(8,128)(2,1)S(1)}, bf16[2,1,3,4,3,8,8,128]{7,6,5,3,4,2,0,1:T(8,128)(2,1)S(1)}) fusion(bf16[2,4,4,3,8,8,768]{6,5,4,2,3,1,0:T(8,128)(2,1)} %get-tuple-element.148, s32[]{:T(128)S(6)} %select_n.12, s32[]{:T(128)S(6)} %add.76), kind=kLoop, calls=%fused_computation.10.clone.1 | loop fusion | bytes 4718600 | tf_op jit(solution)/shard_map/while/body/eval_jaxpr/stack | solution.py:60
  140.4 0.2 maximum_bitcast_fusion.2
  140.7 0.6 fusion.37
  141.3 1.8 %fusion.38 = (f32[2,256]{1,0:T(2,128)S(1)}, f32[2,256,2304]{2,1,0:T(8,128)S(1)}) fusion(bf16[2,2304,128]{2,1,0:T(8,128)(2,1)S(1)} %bitcast.37, bf16[2,256,768]{2,1,0:T(8,128)(2,1)} %get-tuple-element.147, s32[]{:T(128)S(6)} %select_n.12, pred[2,2304]{1,0:T(4,128)(4,1)S(1)} %get-tuple-element.149), kind=kOutput, calls=%fused_computation.29.clone.1 | convolution fusion | flops 305528320 | bytes 6035972 | tf_op jit(solution)/shard_map/while/body/eval_jaxpr/jyh,jvh->jyv/dot_general | solution.py:66
  143.1 0.8 fusion.39
  143.8 1.6 fusion.40
  145.5 0.6 dynamic_slice.20
  146.6 2.2 %dynamic-slice_bitcast_fusion.3 = (bf16[2,1,3,4,3,8,8,128]{7,6,5,3,4,2,0,1:T(8,128)(2,1)S(1)}, bf16[2,1,3,4,3,8,8,128]{7,6,5,3,4,2,0,1:T(8,128)(2,1)S(1)}) fusion(bf16[2,4,4,3,8,8,768]{6,5,4,2,3,1,0:T(8,128)(2,1)} %get-tuple-element.148, s32[]{:T(128)S(6)} %select_n.12, s32[]{:T(128)S(6)} %add.76), kind=kLoop, calls=%fused_computation.10.clone.1 | loop fusion | bytes 4718600 | tf_op jit(solution)/shard_map/while/body/eval_jaxpr/stack | solution.py:60
  148.8 0.2 maximum_bitcast_fusion.2
  149.0 0.6 fusion.37
  149.6 1.8 %fusion.38 = (f32[2,256]{1,0:T(2,128)S(1)}, f32[2,256,2304]{2,1,0:T(8,128)S(1)}) fusion(bf16[2,2304,128]{2,1,0:T(8,128)(2,1)S(1)} %bitcast.37, bf16[2,256,768]{2,1,0:T(8,128)(2,1)} %get-tuple-element.147, s32[]{:T(128)S(6)} %select_n.12, pred[2,2304]{1,0:T(4,128)(4,1)S(1)} %get-tuple-element.149), kind=kOutput, calls=%fused_computation.29.clone.1 | convolution fusion | flops 305528320 | bytes 6035972 | tf_op jit(solution)/shard_map/while/body/eval_jaxpr/jyh,jvh->jyv/dot_general | solution.py:66
  151.4 0.8 fusion.39
  152.2 1.6 fusion.40
  153.8 0.6 dynamic_slice.20
  155.0 2.2 %dynamic-slice_bitcast_fusion.3 = (bf16[2,1,3,4,3,8,8,128]{7,6,5,3,4,2,0,1:T(8,128)(2,1)S(1)}, bf16[2,1,3,4,3,8,8,128]{7,6,5,3,4,2,0,1:T(8,128)(2,1)S(1)}) fusion(bf16[2,4,4,3,8,8,768]{6,5,4,2,3,1,0:T(8,128)(2,1)} %get-tuple-element.148, s32[]{:T(128)S(6)} %select_n.12, s32[]{:T(128)S(6)} %add.76), kind=kLoop, calls=%fused_computation.10.clone.1 | loop fusion | bytes 4718600 | tf_op jit(solution)/shard_map/while/body/eval_jaxpr/stack | solution.py:60
  157.2 0.2 maximum_bitcast_fusion.2
  157.4 0.6 fusion.37
  158.0 1.8 %fusion.38 = (f32[2,256]{1,0:T(2,128)S(1)}, f32[2,256,2304]{2,1,0:T(8,128)S(1)}) fusion(bf16[2,2304,128]{2,1,0:T(8,128)(2,1)S(1)} %bitcast.37, bf16[2,256,768]{2,1,0:T(8,128)(2,1)} %get-tuple-element.147, s32[]{:T(128)S(6)} %select_n.12, pred[2,2304]{1,0:T(4,128)(4,1)S(1)} %get-tuple-element.149), kind=kOutput, calls=%fused_computation.29.clone.1 | convolution fusion | flops 305528320 | bytes 6035972 | tf_op jit(solution)/shard_map/while/body/eval_jaxpr/jyh,jvh->jyv/dot_general | solution.py:66
  159.8 0.8 fusion.39
  160.6 1.6 fusion.40
  162.2 1.7 %copy.5 = bf16[2,256,6,128]{3,2,1,0:T(8,128)(2,1)S(1)} copy(bf16[2,256,6,128]{3,1,0,2:T(8,128)(2,1)} %bitcast.45) | data formatting | bytes 1572864 | tf_op jit(solution)/shard_map/transpose | solution.py:82
  163.9 1.8 %reshape_transpose_reshape.7 = bf16[8,8,8,768]{3,2,1,0:T(8,128)(2,1)} reshape(bf16[2,256,6,128]{3,2,1,0:T(8,128)(2,1)S(1)} %copy.5) | data formatting | bytes 1572864 | tf_op jit(solution)/shard_map/reshape;transpose;reshape | solution.py:85
  (6 shorter events, 0.0 us)
Async XLA Ops:
  0.0 27.5 %copy-start = (bf16[8,8,8,768]{3,2,1,0:T(8,128)(2,1)S(1)}, bf16[8,8,8,768]{3,2,1,0:T(8,128)(2,1)}, u32[]{:S(2)}) copy-start(bf16[8,8,8,768]{3,2,1,0:T(8,128)(2,1)} %param.6) | copy-start | bytes 2359300
  0.0 27.5 %copy-start.1 = (bf16[8,8,8,768]{3,2,1,0:T(8,128)(2,1)S(1)}, bf16[8,8,8,768]{3,2,1,0:T(8,128)(2,1)}, u32[]{:S(2)}) copy-start(bf16[8,8,8,768]{3,2,1,0:T(8,128)(2,1)} %param.7) | copy-start | bytes 2359300
  1.6 21.7 %collective-permute-start = (bf16[2,1,4,1,8,8,768]{6,5,4,2,3,1,0:T(8,128)(2,1)S(1)}, bf16[2,1,4,1,8,8,768]{6,5,4,2,3,1,0:T(8,128)(2,1)S(1)}, u32[]{:S(2)}, u32[]{:S(2)}) collective-permute-start(bf16[2,1,4,1,8,8,768]{6,5,4,2,3,1,0:T(8,128)(2,1)S(1)} %get-tuple-element.71), channel_id=1, source_target_pairs={{0,4},{4,8},{8,12},{1,5},{5,9},{9,13},{2,6},{6,10},{10,14},{3,7},{... | collective-permute-start | bytes 2359304 | tf_op jit(solution)/shard_map/ppermute | solution.py:22
  6.6 20.9 %collective-permute-start.1 = (bf16[2,1,4,1,8,8,768]{6,5,4,2,3,1,0:T(8,128)(2,1)S(1)}, bf16[2,1,4,1,8,8,768]{6,5,4,2,3,1,0:T(8,128)(2,1)S(1)}, u32[]{:S(2)}, u32[]{:S(2)}) collective-permute-start(bf16[2,1,4,1,8,8,768]{6,5,4,2,3,1,0:T(8,128)(2,1)S(1)} %get-tuple-element.72), channel_id=1, source_target_pairs={{4,0},{8,4},{12,8},{5,1},{9,5},{13,9},{6,2},{10,6},{14,10},{7,3},{... | collective-permute-start | bytes 2359304 | tf_op jit(solution)/shard_map/ppermute | solution.py:24
  29.4 69.9 %collective-permute-start.2 = (bf16[2,4,4,1,8,8,768]{6,5,4,2,3,1,0:T(8,128)(2,1)}, bf16[2,4,4,1,8,8,768]{6,5,4,2,3,1,0:T(8,128)(2,1)}, u32[]{:S(2)}, u32[]{:S(2)}) collective-permute-start(bf16[2,4,4,1,8,8,768]{6,5,4,2,3,1,0:T(8,128)(2,1)} %pad_maximum_fusion.1), channel_id=1, source_target_pairs={{0,2},{1,3},{4,6},{5,7},{8,10},{9,11},{12,14},{13,15},{16,18},{17,... | collective-permute-start | bytes 9437192 | tf_op jit(solution)/shard_map/ppermute | solution.py:22
  34.4 70.6 %collective-permute-start.3 = (bf16[2,4,4,1,8,8,768]{6,5,4,2,3,1,0:T(8,128)(2,1)}, bf16[2,4,4,1,8,8,768]{6,5,4,2,3,1,0:T(8,128)(2,1)}, u32[]{:S(2)}, u32[]{:S(2)}) collective-permute-start(bf16[2,4,4,1,8,8,768]{6,5,4,2,3,1,0:T(8,128)(2,1)} %pad_maximum_fusion.1), channel_id=1, source_target_pairs={{2,0},{3,1},{6,4},{7,5},{10,8},{11,9},{14,12},{15,13},{18,16},{19,... | collective-permute-start | bytes 9437192 | tf_op jit(solution)/shard_map/ppermute | solution.py:24
where the time goes:
time: 166 us
  waiting for transfers between devices  88.6 us (53%)
  local copies, waits for them, and re-layouts  23.7 us (14%)
  matrix products  20.5 us (12%)
  other arithmetic  16.6 us (10%)
  starting transfers between devices  12.6 us (8%)
  loops' own time  3.57 us (2%)
    ppermute x2, waiting for transfers between devices, padded(): lax.ppermute(tail, axis, [(i, (i + 1) % count) for i in range(ends)])  78.7 us
    another operation x6, local copies, waits for them, and re-layouts, one_head(): key_groups = jnp.stack((head_grid[:, 0:3], head_grid[:, 1:4]), 1)  13.2 us
    dot_general x6, matrix products, one_head(): jnp.einsum('jyh,jvh->jyv', head_queries, key_groups[0], preferred_element...  10.8 us
    ppermute x2, starting transfers between devices, padded(): lax.ppermute(tail, axis, [(i, (i + 1) % count) for i in range(ends)])  10 us
    ppermute x2, waiting for transfers between devices, padded(): lax.ppermute(head, axis, [((i + 1) % count, i) for i in range(ends)])  9.9 us
    dot_general x6, matrix products, one_head(): jnp.einsum('git,gth->gih', rounded_length, key_groups[1], preferred_eleme...  9.7 us
    concatenate x2, other arithmetic, padded(): jnp.concatenate([lax.ppermute(tail, axis, [(i, (i + 1) % count) for i in...  8.82 us
    reduce_sum x6, other arithmetic, one_head(): row_total = jnp.sum(weights, axis=-1, keepdims=True)  4.71 us
  transfers between devices with their start and end apart: 4, of which 4 were waited for; matrix products, arithmetic and copies ran while one was open for 0% of the time, Pallas kernels for 0%

commit v1 on v0

v1 whole, which is shorter than its diff:
```python
import functools
import math

import jax
import jax.numpy as jnp
from jax import lax
from jax.experimental import pallas as pl
from jax.experimental.pallas import tpu as pltpu
from jax.sharding import PartitionSpec as P

HD = 128
TF = 4
TR = 8
TC = 8


def shift(cells, axis, forward):
    count = lax.axis_size(axis)
    if forward:
        pairs = [(i, i + 1) for i in range(count - 1)]
    else:
        pairs = [(i + 1, i) for i in range(count - 1)]
    return lax.ppermute(cells, axis, pairs)


def attention_kernel(bias_ref, q_ref, k_ref, v_ref, o_ref, *, tile_frames, score_scale):
    for j in range(tile_frames):
        q = q_ref[j]
        k = k_ref[:, j : j + 3].reshape(-1, HD)
        v = v_ref[:, j : j + 3].reshape(-1, HD)
        s = lax.dot_general(q, k, (((1,), (1,)), ((), ())), preferred_element_type=jnp.float32)
        s = s * score_scale + bias_ref[j]
        m = jnp.max(s, axis=1, keepdims=True)
        p = jnp.exp(s - m)
        l = jnp.sum(p, axis=1, keepdims=True)
        o = jnp.dot(p.astype(jnp.bfloat16), v, preferred_element_type=jnp.float32)
        o_ref[j] = (o / l).astype(o_ref.dtype)


def per_device(query, keys, values):
    frames, rows, columns, features = query.shape
    tile_frames = frames // TF
    tile_size = TF * TR * TC
    heads_here = features // HD
    score_scale = 1.0 / math.sqrt(HD)

    def tiles(x):
        return x.reshape(tile_frames, tile_size, features)

    kv = (tiles(keys), tiles(values))
    above = shift(kv, "row", True)
    below = shift(kv, "row", False)
    own_prev = shift(tuple(x[tile_frames - 1] for x in kv), "frame", True)
    own_next = shift(tuple(x[0] for x in kv), "frame", False)
    diag_prev = shift(
        tuple(jnp.stack((a[tile_frames - 1], b[tile_frames - 1])) for a, b in zip(above, below)),
        "frame",
        True,
    )
    diag_next = shift(tuple(jnp.stack((a[0], b[0])) for a, b in zip(above, below)), "frame", False)

    def window(i):
        middle = jnp.concatenate((own_prev[i][None], kv[i], own_next[i][None]), 0)
        top = jnp.concatenate((diag_prev[i][0][None], above[i], diag_next[i][0][None]), 0)
        bottom = jnp.concatenate((diag_prev[i][1][None], below[i], diag_next[i][1][None]), 0)
        return jnp.stack((top, middle, bottom))

    key_window = window(0)
    value_window = window(1)

    frame_index = lax.axis_index("frame")
    row_index = lax.axis_index("row")
    offsets = jnp.arange(3, dtype=jnp.int32) - 1
    global_frames = frame_index * tile_frames + jnp.arange(tile_frames + 2, dtype=jnp.int32) - 1
    frame_ok = (global_frames >= 0) & (global_frames < tile_frames * lax.axis_size("frame"))
    row_ids = row_index + offsets
    row_ok = (row_ids >= 0) & (row_ids < lax.axis_size("row"))
    bias_rows = []
    for j in range(tile_frames):
        ok = row_ok[:, None] & frame_ok[None, j : j + 3]
        ok = jnp.broadcast_to(ok[:, :, None], (3, 3, tile_size)).reshape(1, 9 * tile_size)
        bias_rows.append(jnp.where(ok, 0.0, -jnp.inf).astype(jnp.float32))
    bias = jnp.stack(bias_rows)

    q = tiles(query)
    kernel = functools.partial(
        attention_kernel, tile_frames=tile_frames, score_scale=score_scale
    )
    window_block = (3, tile_frames + 2, tile_size, HD)
    out = pl.pallas_call(
        kernel,
        grid=(heads_here,),
        in_specs=[
            pl.BlockSpec((tile_frames, 1, 9 * tile_size), lambda h: (0, 0, 0)),
            pl.BlockSpec((tile_frames, tile_size, HD), lambda h: (0, 0, h)),
            pl.BlockSpec(window_block, lambda h: (0, 0, 0, h)),
            pl.BlockSpec(window_block, lambda h: (0, 0, 0, h)),
        ],
        out_specs=pl.BlockSpec((tile_frames, tile_size, HD), lambda h: (0, 0, h)),
        out_shape=jax.ShapeDtypeStruct(q.shape, query.dtype),
        compiler_params=pltpu.CompilerParams(vmem_limit_bytes=48 * 1024 * 1024),
    )(bias, q, key_window, value_window)
    return out.reshape(frames, rows, columns, features)


def solution(mesh):
    return jax.shard_map(
        per_device,
        mesh=mesh,
        in_specs=(
            P(("clips", "frame"), "row", None, "head"),
            P(("clips", "frame"), "row", None, "head"),
            P(("clips", "frame"), "row", None, "head"),
        ),
        out_specs=P(("clips", "frame"), "row", None, "head"),
        check_vma=False,
    )
```

time: 166 us -> 89.4 us (0.54)
  waiting for transfers between devices: 88.6 us -> 28.9 us
  matrix products: 20.5 us -> 0 us
  starting transfers between devices: 12.6 us -> 32 us
  local copies, waits for them, and re-layouts: 23.7 us -> 5.39 us
  Pallas kernels: 0 us -> 15.8 us
  other arithmetic: 16.6 us -> 6.4 us
  loops' own time: 3.57 us -> 0 us
    ppermute x4 -> x12, waiting for transfers between devices: 88.6 us -> 28.9 us  [shift(): return lax.ppermute(cells, axis, pairs)]
    dot_general x12 -> x0, matrix products: 20.5 us -> none  [the longest x6 10.8 us: one_head(): jnp.einsum('jyh,jvh->jyv', head_queries, key_groups[0], preferred_element...]
    ppermute x4 -> x12, starting transfers between devices: 12.6 us -> 32 us  [shift(): return lax.ppermute(cells, axis, pairs)]
    pallas_call x0 -> x1, Pallas kernels: none -> 15.8 us  [per_device(): pl.pallas_call(kernel, grid=(heads_here,), in_specs=[pl.BlockSpec((tile_f...]
    another operation x7 -> x0, local copies, waits for them, and re-layouts: 14.9 us -> none  [the longest x6 13.2 us: one_head(): key_groups = jnp.stack((head_grid[:, 0:3], head_grid[:, 1:4]), 1)]
    concatenate x2 -> x0, other arithmetic: 8.82 us -> none  [padded(): jnp.concatenate([lax.ppermute(tail, axis, [(i, (i + 1) % count) for i in...]
    reduce_sum x6 -> x0, other arithmetic: 4.71 us -> none  [one_head(): row_total = jnp.sum(weights, axis=-1, keepdims=True)]
    another operation x1 -> x11, other arithmetic: 1.61 us -> 6.24 us  [the longest x6 5.21 us: window(): return jnp.stack((top, middle, bottom))]
  transfers between devices with their start and end apart: 4 -> 12, of which waited for: 4 -> 8; matrix products, arithmetic and copies ran while one was open for 0% -> 12% of each run, Pallas kernels for 0% -> 0%
where the time goes in v1:
time: 89.4 us; the launch traced here: 88.8 us
  starting transfers between devices  32 us (36%)
  waiting for transfers between devices  28.9 us (32%)
  Pallas kernels  15.8 us (18%)
  other arithmetic  6.4 us (7%)
  local copies, waits for them, and re-layouts  5.39 us (6%)
    ppermute x12, starting transfers between devices, shift(): return lax.ppermute(cells, axis, pairs)  32 us
    ppermute x12, waiting for transfers between devices, shift(): return lax.ppermute(cells, axis, pairs)  28.9 us
    pallas_call x1, Pallas kernels, per_device(): pl.pallas_call(kernel, grid=(heads_here,), in_specs=[pl.BlockSpec((tile_f...  15.8 us
    another operation x6, other arithmetic, window(): return jnp.stack((top, middle, bottom))  5.21 us
    slice x2, local copies, waits for them, and re-layouts, per_device(): own_prev = shift(tuple((x[tile_frames - 1] for x in kv)), 'frame', True)  3.03 us
  transfers between devices with their start and end apart: 12, of which 8 were waited for; matrix products, arithmetic and copies ran while one was open for 12% of the time, Pallas kernels for 0%

profile of v1, /device:TPU:0, one launch (start us, length us, event | category | flops | bytes accessed | tf_op | source)
XLA Modules:
  0.0 88.8 jit_solution(5687524448828771331)
XLA Ops:
  0.0 0.0 copy-start.2
  0.0 0.0 copy-start.1
  0.0 5.0 %collective-permute-start.6 = (bf16[2,256,768]{2,1,0:T(8,128)(2,1)}, bf16[2,256,768]{2,1,0:T(8,128)(2,1)S(1)}, u32[]{:S(2)}, u32[]{:S(2)}) collective-permute-start(bf16[2,256,768]{2,1,0:T(8,128)(2,1)} %bitcast.25), channel_id=1, source_target_pairs={{0,2},{1,3},{4,6},{5,7},{8,10},{9,11},{12,14},{13,15},{16,18},{17,... | collective-permute-start | bytes 2359304 | tf_op jit(solution)/shard_map/ppermute | solution.py:23
  5.1 1.3 %collective-permute-start.7 = (bf16[2,256,768]{2,1,0:T(8,128)(2,1)}, bf16[2,256,768]{2,1,0:T(8,128)(2,1)S(1)}, u32[]{:S(2)}, u32[]{:S(2)}) collective-permute-start(bf16[2,256,768]{2,1,0:T(8,128)(2,1)} %bitcast.26), channel_id=1, source_target_pairs={{2,0},{3,1},{6,4},{7,5},{10,8},{11,9},{14,12},{15,13},{18,16},{19,... | collective-permute-start | bytes 2359304 | tf_op jit(solution)/shard_map/ppermute | solution.py:23
  6.4 2.1 %fusion.2 = (bf16[4,8,8,768]{3,2,1,0:T(8,128)(2,1)}, bf16[4,8,8,768]{3,2,1,0:T(8,128)(2,1)}) fusion(bf16[8,8,8,768]{3,2,1,0:T(8,128)(2,1)} %param.5), kind=kLoop, calls=%fused_computation.19 | loop fusion | bytes 1572864 | tf_op jit(solution)/shard_map/slice | solution.py:53
  8.4 4.2 %collective-permute-start.10 = (bf16[256,768]{1,0:T(8,128)(2,1)}, bf16[256,768]{1,0:T(8,128)(2,1)}, u32[]{:S(2)}, u32[]{:S(2)}) collective-permute-start(bf16[256,768]{1,0:T(8,128)(2,1)} %bitcast.11), channel_id=1, source_target_pairs={{0,4},{4,8},{8,12},{1,5},{5,9},{9,13},{2,6},{6,10},{10,14},{3,7},{... | collective-permute-start | bytes 1179656 | tf_op jit(solution)/shard_map/ppermute | solution.py:23
  12.7 1.3 %collective-permute-start.11 = (bf16[256,768]{1,0:T(8,128)(2,1)}, bf16[256,768]{1,0:T(8,128)(2,1)}, u32[]{:S(2)}, u32[]{:S(2)}) collective-permute-start(bf16[256,768]{1,0:T(8,128)(2,1)} %bitcast.13), channel_id=1, source_target_pairs={{4,0},{8,4},{12,8},{5,1},{9,5},{13,9},{6,2},{10,6},{14,10},{7,3},{... | collective-permute-start | bytes 1179656 | tf_op jit(solution)/shard_map/ppermute | solution.py:23
  13.9 0.0 copy-done.2
  14.0 0.9 %fusion.7 = (bf16[4,8,8,768]{3,2,1,0:T(8,128)(2,1)}, bf16[4,8,8,768]{3,2,1,0:T(8,128)(2,1)}) fusion(bf16[8,8,8,768]{3,2,1,0:T(8,128)(2,1)S(1)} %copy-done.2), kind=kLoop, calls=%fused_computation.24 | loop fusion | bytes 1572864 | tf_op jit(solution)/shard_map/slice | solution.py:53
  14.9 4.6 %collective-permute-start.4 = (bf16[256,768]{1,0:T(8,128)(2,1)}, bf16[256,768]{1,0:T(8,128)(2,1)S(1)}, u32[]{:S(2)}, u32[]{:S(2)}) collective-permute-start(bf16[256,768]{1,0:T(8,128)(2,1)} %bitcast.3), channel_id=1, source_target_pairs={{0,4},{4,8},{8,12},{1,5},{5,9},{9,13},{2,6},{6,10},{10,14},{3,7},{... | collective-permute-start | bytes 1179656 | tf_op jit(solution)/shard_map/ppermute | solution.py:23
  19.5 0.1 fusion.10
  19.6 0.1 and_select_fusion.1
  19.6 0.1 broadcast_in_dim.40
  19.7 0.6 select_n.34
  20.3 0.1 broadcast_in_dim.41
  20.4 0.6 select_n.36
  21.0 0.7 collective-permute-done.10
  21.7 1.3 %collective-permute-start.5 = (bf16[256,768]{1,0:T(8,128)(2,1)}, bf16[256,768]{1,0:T(8,128)(2,1)S(1)}, u32[]{:S(2)}, u32[]{:S(2)}) collective-permute-start(bf16[256,768]{1,0:T(8,128)(2,1)} %bitcast.33), channel_id=1, source_target_pairs={{4,0},{8,4},{12,8},{5,1},{9,5},{13,9},{6,2},{10,6},{14,10},{7,3},{... | collective-permute-start | bytes 1179656 | tf_op jit(solution)/shard_map/ppermute | solution.py:23
  23.0 0.7 pad_maximum_fusion.6.bias_ref
  23.7 2.0 %collective-permute-done.11 = bf16[256,768]{1,0:T(8,128)(2,1)} collective-permute-done((bf16[256,768]{1,0:T(8,128)(2,1)}, bf16[256,768]{1,0:T(8,128)(2,1)}, u32[]{:S(2)}, u32[]{:S(2)}) %collective-permute-start.11) | collective-permute-done | bytes 393248 | tf_op jit(solution)/shard_map/ppermute | solution.py:23
  25.8 4.3 %collective-permute-start = (bf16[2,256,768]{2,1,0:T(8,128)(2,1)S(1)}, bf16[2,256,768]{2,1,0:T(8,128)(2,1)S(1)}, u32[]{:S(2)}, u32[]{:S(2)}) collective-permute-start(bf16[2,256,768]{2,1,0:T(8,128)(2,1)S(1)} %bitcast.28), channel_id=1, source_target_pairs={{0,2},{1,3},{4,6},{5,7},{8,10},{9,11},{12,14},{13,15},{16,18},{17,... | collective-permute-start | bytes 2359304 | tf_op jit(solution)/shard_map/ppermute | solution.py:23
  30.1 0.0 copy-done.1
  30.1 1.3 %maximum_bitcast_fusion.4 = bf16[1,4,256,768]{3,2,1,0:T(8,128)(2,1)S(1)} fusion(bf16[1,256,768]{2,1,0:T(8,128)(2,1)} %bitcast.14, bf16[2,256,768]{2,1,0:T(8,128)(2,1)S(1)} %bitcast.27, bf16[1,256,768]{2,1,0:T(8,128)(2,1)} %bitcast.12), kind=kLoop, calls=%fused_computation.6 | loop fusion | flops 1572864 | bytes 3145728 | tf_op jit(solution)/shard_map/stack | solution.py:66
  31.4 0.0 collective-permute-done.4
  31.4 1.3 %collective-permute-start.1 = (bf16[2,256,768]{2,1,0:T(8,128)(2,1)S(1)}, bf16[2,256,768]{2,1,0:T(8,128)(2,1)S(1)}, u32[]{:S(2)}, u32[]{:S(2)}) collective-permute-start(bf16[2,256,768]{2,1,0:T(8,128)(2,1)S(1)} %bitcast.29), channel_id=1, source_target_pairs={{2,0},{3,1},{6,4},{7,5},{10,8},{11,9},{14,12},{15,13},{18,16},{19,... | collective-permute-start | bytes 2359304 | tf_op jit(solution)/shard_map/ppermute | solution.py:23
  32.7 0.7 collective-permute-done.5
  33.5 0.2 maximum_bitcast_fusion.1
  33.7 0.0 collective-permute-done.6
  33.7 0.1 fusion.3
  33.7 0.0 collective-permute-done.7
  33.7 0.1 fusion.4
  33.8 0.1 pad_maximum_fusion.4
  33.9 3.1 %collective-permute-start.8 = (bf16[2,256,768]{2,1,0:T(8,128)(2,1)S(1)}, bf16[2,256,768]{2,1,0:T(8,128)(2,1)S(1)}, u32[]{:S(2)}, u32[]{:S(2)}) collective-permute-start(bf16[2,256,768]{2,1,0:T(8,128)(2,1)S(1)} %pad_maximum_fusion.4), channel_id=1, source_target_pairs={{0,4},{4,8},{8,12},{1,5},{5,9},{9,13},{2,6},{6,10},{10,14},{3,7},{... | collective-permute-start | bytes 2359304 | tf_op jit(solution)/shard_map/ppermute | solution.py:23
  37.0 0.1 pad_maximum_fusion.5
  37.1 1.3 %collective-permute-start.9 = (bf16[2,256,768]{2,1,0:T(8,128)(2,1)S(1)}, bf16[2,256,768]{2,1,0:T(8,128)(2,1)S(1)}, u32[]{:S(2)}, u32[]{:S(2)}) collective-permute-start(bf16[2,256,768]{2,1,0:T(8,128)(2,1)S(1)} %pad_maximum_fusion.5), channel_id=1, source_target_pairs={{4,0},{8,4},{12,8},{5,1},{9,5},{13,9},{6,2},{10,6},{14,10},{7,3},{... | collective-permute-start | bytes 2359304 | tf_op jit(solution)/shard_map/ppermute | solution.py:23
  38.4 6.2 %collective-permute-done = bf16[2,256,768]{2,1,0:T(8,128)(2,1)S(1)} collective-permute-done((bf16[2,256,768]{2,1,0:T(8,128)(2,1)S(1)}, bf16[2,256,768]{2,1,0:T(8,128)(2,1)S(1)}, u32[]{:S(2)}, u32[]{:S(2)}) %collective-permute-start) | collective-permute-done | bytes 786464 | tf_op jit(solution)/shard_map/ppermute | solution.py:23
  44.5 0.1 fusion.8
  44.6 5.4 %collective-permute-done.1 = bf16[2,256,768]{2,1,0:T(8,128)(2,1)S(1)} collective-permute-done((bf16[2,256,768]{2,1,0:T(8,128)(2,1)S(1)}, bf16[2,256,768]{2,1,0:T(8,128)(2,1)S(1)}, u32[]{:S(2)}, u32[]{:S(2)}) %collective-permute-start.1) | collective-permute-done | bytes 786464 | tf_op jit(solution)/shard_map/ppermute | solution.py:23
  50.0 0.1 fusion.9
  50.1 0.1 pad_maximum_fusion.2
  50.2 3.1 %collective-permute-start.2 = (bf16[2,256,768]{2,1,0:T(8,128)(2,1)S(1)}, bf16[2,256,768]{2,1,0:T(8,128)(2,1)S(1)}, u32[]{:S(2)}, u32[]{:S(2)}) collective-permute-start(bf16[2,256,768]{2,1,0:T(8,128)(2,1)S(1)} %pad_maximum_fusion.2), channel_id=1, source_target_pairs={{0,4},{4,8},{8,12},{1,5},{5,9},{9,13},{2,6},{6,10},{10,14},{3,7},{... | collective-permute-start | bytes 2359304 | tf_op jit(solution)/shard_map/ppermute | solution.py:23
  53.2 0.1 pad_maximum_fusion.3
  53.3 1.3 %collective-permute-start.3 = (bf16[2,256,768]{2,1,0:T(8,128)(2,1)S(1)}, bf16[2,256,768]{2,1,0:T(8,128)(2,1)S(1)}, u32[]{:S(2)}, u32[]{:S(2)}) collective-permute-start(bf16[2,256,768]{2,1,0:T(8,128)(2,1)S(1)} %pad_maximum_fusion.3), channel_id=1, source_target_pairs={{4,0},{8,4},{12,8},{5,1},{9,5},{13,9},{6,2},{10,6},{14,10},{7,3},{... | collective-permute-start | bytes 2359304 | tf_op jit(solution)/shard_map/ppermute | solution.py:23
  54.6 0.0 collective-permute-done.8
  54.6 0.1 fusion
  54.7 0.7 collective-permute-done.9
  55.4 0.1 fusion.1
  55.4 0.4 maximum_bitcast_fusion.3
  55.8 11.4 %collective-permute-done.2 = bf16[2,256,768]{2,1,0:T(8,128)(2,1)S(1)} collective-permute-done((bf16[2,256,768]{2,1,0:T(8,128)(2,1)S(1)}, bf16[2,256,768]{2,1,0:T(8,128)(2,1)S(1)}, u32[]{:S(2)}, u32[]{:S(2)}) %collective-permute-start.2) | collective-permute-done | bytes 786464 | tf_op jit(solution)/shard_map/ppermute | solution.py:23
  67.2 0.1 fusion.5
  67.3 2.4 %pad_maximum_fusion.1.v_ref = bf16[3,4,256,768]{3,2,1,0:T(8,128)(2,1)} fusion(bf16[1,4,256,768]{3,2,1,0:T(8,128)(2,1)S(1)} %get-tuple-element.33, bf16[1,4,256,768]{3,2,1,0:T(8,128)(2,1)S(1)} %maximum_bitcast_fusion.4, bf16[1,4,256,768]{3,2,1,0:T(8,128)(2,1)S(1)} %get-tuple-element.32), kind=kLoop, calls=%fused_computation.1 | loop fusion | flops 4718592 | bytes 9437184 | tf_op jit(solution)/shard_map/stack | solution.py:66
  69.7 1.7 %collective-permute-done.3 = bf16[2,256,768]{2,1,0:T(8,128)(2,1)S(1)} collective-permute-done((bf16[2,256,768]{2,1,0:T(8,128)(2,1)S(1)}, bf16[2,256,768]{2,1,0:T(8,128)(2,1)S(1)}, u32[]{:S(2)}, u32[]{:S(2)}) %collective-permute-start.3) | collective-permute-done | bytes 786464 | tf_op jit(solution)/shard_map/ppermute | solution.py:23
  71.5 0.1 fusion.6
  71.5 0.4 maximum_bitcast_fusion
  71.9 0.0 copy-start
  71.9 0.6 pad_maximum_fusion.k_ref
  72.5 0.6 copy-done
  73.0 15.8 %shard_map.37 = bf16[2,256,768]{2,1,0:T(8,128)(2,1)} custom-call(f32[2,1,2304]{2,1,0:T(1,128)S(1)} %pad_maximum_fusion.6.bias_ref, bf16[2,256,768]{2,1,0:T(8,128)(2,1)S(1)} %bitcast.24, bf16[3,4,256,768]{3,2,1,0:T(8,128)(2,1)S(1)} %pad_maximum_fusion.k_ref, bf16[3,4,256,768]{3,2,1,0:T(8,128)(2,1)} %pad_maximum_fusion.1.v_ref), custom_call_target="tpu_custom_call" | custom-call | tf_op jit(solution)/shard_map/pallas_call | solution.py:90
  (1 shorter events, 0.0 us)
Async XLA Ops:
  0.0 13.9 %copy-start.2 = (bf16[8,8,8,768]{3,2,1,0:T(8,128)(2,1)S(1)}, bf16[8,8,8,768]{3,2,1,0:T(8,128)(2,1)}, u32[]{:S(2)}) copy-start(bf16[8,8,8,768]{3,2,1,0:T(8,128)(2,1)} %param.4) | copy-start | bytes 2359300
  0.0 30.1 %copy-start.1 = (bf16[8,8,8,768]{3,2,1,0:T(8,128)(2,1)S(1)}, bf16[8,8,8,768]{3,2,1,0:T(8,128)(2,1)}, u32[]{:S(2)}) copy-start(bf16[8,8,8,768]{3,2,1,0:T(8,128)(2,1)} %param.5) | copy-start | bytes 2359300
  0.0 33.7 %collective-permute-start.6 = (bf16[2,256,768]{2,1,0:T(8,128)(2,1)}, bf16[2,256,768]{2,1,0:T(8,128)(2,1)S(1)}, u32[]{:S(2)}, u32[]{:S(2)}) collective-permute-start(bf16[2,256,768]{2,1,0:T(8,128)(2,1)} %bitcast.25), channel_id=1, source_target_pairs={{0,2},{1,3},{4,6},{5,7},{8,10},{9,11},{12,14},{13,15},{16,18},{17,... | collective-permute-start | bytes 2359304 | tf_op jit(solution)/shard_map/ppermute | solution.py:23
  5.1 28.7 %collective-permute-start.7 = (bf16[2,256,768]{2,1,0:T(8,128)(2,1)}, bf16[2,256,768]{2,1,0:T(8,128)(2,1)S(1)}, u32[]{:S(2)}, u32[]{:S(2)}) collective-permute-start(bf16[2,256,768]{2,1,0:T(8,128)(2,1)} %bitcast.26), channel_id=1, source_target_pairs={{2,0},{3,1},{6,4},{7,5},{10,8},{11,9},{14,12},{15,13},{18,16},{19,... | collective-permute-start | bytes 2359304 | tf_op jit(solution)/shard_map/ppermute | solution.py:23
  8.4 13.3 %collective-permute-start.10 = (bf16[256,768]{1,0:T(8,128)(2,1)}, bf16[256,768]{1,0:T(8,128)(2,1)}, u32[]{:S(2)}, u32[]{:S(2)}) collective-permute-start(bf16[256,768]{1,0:T(8,128)(2,1)} %bitcast.11), channel_id=1, source_target_pairs={{0,4},{4,8},{8,12},{1,5},{5,9},{9,13},{2,6},{6,10},{10,14},{3,7},{... | collective-permute-start | bytes 1179656 | tf_op jit(solution)/shard_map/ppermute | solution.py:23
  12.7 13.1 %collective-permute-start.11 = (bf16[256,768]{1,0:T(8,128)(2,1)}, bf16[256,768]{1,0:T(8,128)(2,1)}, u32[]{:S(2)}, u32[]{:S(2)}) collective-permute-start(bf16[256,768]{1,0:T(8,128)(2,1)} %bitcast.13), channel_id=1, source_target_pairs={{4,0},{8,4},{12,8},{5,1},{9,5},{13,9},{6,2},{10,6},{14,10},{7,3},{... | collective-permute-start | bytes 1179656 | tf_op jit(solution)/shard_map/ppermute | solution.py:23
  14.9 16.5 %collective-permute-start.4 = (bf16[256,768]{1,0:T(8,128)(2,1)}, bf16[256,768]{1,0:T(8,128)(2,1)S(1)}, u32[]{:S(2)}, u32[]{:S(2)}) collective-permute-start(bf16[256,768]{1,0:T(8,128)(2,1)} %bitcast.3), channel_id=1, source_target_pairs={{0,4},{4,8},{8,12},{1,5},{5,9},{9,13},{2,6},{6,10},{10,14},{3,7},{... | collective-permute-start | bytes 1179656 | tf_op jit(solution)/shard_map/ppermute | solution.py:23
  21.7 11.8 %collective-permute-start.5 = (bf16[256,768]{1,0:T(8,128)(2,1)}, bf16[256,768]{1,0:T(8,128)(2,1)S(1)}, u32[]{:S(2)}, u32[]{:S(2)}) collective-permute-start(bf16[256,768]{1,0:T(8,128)(2,1)} %bitcast.33), channel_id=1, source_target_pairs={{4,0},{8,4},{12,8},{5,1},{9,5},{13,9},{6,2},{10,6},{14,10},{7,3},{... | collective-permute-start | bytes 1179656 | tf_op jit(solution)/shard_map/ppermute | solution.py:23
  25.8 18.8 %collective-permute-start = (bf16[2,256,768]{2,1,0:T(8,128)(2,1)S(1)}, bf16[2,256,768]{2,1,0:T(8,128)(2,1)S(1)}, u32[]{:S(2)}, u32[]{:S(2)}) collective-permute-start(bf16[2,256,768]{2,1,0:T(8,128)(2,1)S(1)} %bitcast.28), channel_id=1, source_target_pairs={{0,2},{1,3},{4,6},{5,7},{8,10},{9,11},{12,14},{13,15},{16,18},{17,... | collective-permute-start | bytes 2359304 | tf_op jit(solution)/shard_map/ppermute | solution.py:23
  31.4 18.6 %collective-permute-start.1 = (bf16[2,256,768]{2,1,0:T(8,128)(2,1)S(1)}, bf16[2,256,768]{2,1,0:T(8,128)(2,1)S(1)}, u32[]{:S(2)}, u32[]{:S(2)}) collective-permute-start(bf16[2,256,768]{2,1,0:T(8,128)(2,1)S(1)} %bitcast.29), channel_id=1, source_target_pairs={{2,0},{3,1},{6,4},{7,5},{10,8},{11,9},{14,12},{15,13},{18,16},{19,... | collective-permute-start | bytes 2359304 | tf_op jit(solution)/shard_map/ppermute | solution.py:23
  33.9 20.7 %collective-permute-start.8 = (bf16[2,256,768]{2,1,0:T(8,128)(2,1)S(1)}, bf16[2,256,768]{2,1,0:T(8,128)(2,1)S(1)}, u32[]{:S(2)}, u32[]{:S(2)}) collective-permute-start(bf16[2,256,768]{2,1,0:T(8,128)(2,1)S(1)} %pad_maximum_fusion.4), channel_id=1, source_target_pairs={{0,4},{4,8},{8,12},{1,5},{5,9},{9,13},{2,6},{6,10},{10,14},{3,7},{... | collective-permute-start | bytes 2359304 | tf_op jit(solution)/shard_map/ppermute | solution.py:23
  37.1 18.3 %collective-permute-start.9 = (bf16[2,256,768]{2,1,0:T(8,128)(2,1)S(1)}, bf16[2,256,768]{2,1,0:T(8,128)(2,1)S(1)}, u32[]{:S(2)}, u32[]{:S(2)}) collective-permute-start(bf16[2,256,768]{2,1,0:T(8,128)(2,1)S(1)} %pad_maximum_fusion.5), channel_id=1, source_target_pairs={{4,0},{8,4},{12,8},{5,1},{9,5},{13,9},{6,2},{10,6},{14,10},{7,3},{... | collective-permute-start | bytes 2359304 | tf_op jit(solution)/shard_map/ppermute | solution.py:23
  50.2 17.1 %collective-permute-start.2 = (bf16[2,256,768]{2,1,0:T(8,128)(2,1)S(1)}, bf16[2,256,768]{2,1,0:T(8,128)(2,1)S(1)}, u32[]{:S(2)}, u32[]{:S(2)}) collective-permute-start(bf16[2,256,768]{2,1,0:T(8,128)(2,1)S(1)} %pad_maximum_fusion.2), channel_id=1, source_target_pairs={{0,4},{4,8},{8,12},{1,5},{5,9},{9,13},{2,6},{6,10},{10,14},{3,7},{... | collective-permute-start | bytes 2359304 | tf_op jit(solution)/shard_map/ppermute | solution.py:23
  53.3 18.2 %collective-permute-start.3 = (bf16[2,256,768]{2,1,0:T(8,128)(2,1)S(1)}, bf16[2,256,768]{2,1,0:T(8,128)(2,1)S(1)}, u32[]{:S(2)}, u32[]{:S(2)}) collective-permute-start(bf16[2,256,768]{2,1,0:T(8,128)(2,1)S(1)} %pad_maximum_fusion.3), channel_id=1, source_target_pairs={{4,0},{8,4},{12,8},{5,1},{9,5},{13,9},{6,2},{10,6},{14,10},{7,3},{... | collective-permute-start | bytes 2359304 | tf_op jit(solution)/shard_map/ppermute | solution.py:23
  71.9 1.1 %copy-start = (bf16[8,8,8,768]{3,2,1,0:T(8,128)(2,1)S(1)}, bf16[8,8,8,768]{3,2,1,0:T(8,128)(2,1)}, u32[]{:S(2)}) copy-start(bf16[8,8,8,768]{3,2,1,0:T(8,128)(2,1)} %param.3) | copy-start | bytes 2359300
